TPU v7x, 128 devices: a whole 4x4x4 slice. The times are simulated.
128 devices in a mesh: dp: 8 (over x_lo, y), expert: 16 (over x_hi, z, core).
Axes of the slice: x: 4 (x_hi: 2, x_lo: 2; x = x_hi * 2 + x_lo), y: 4, z: 4, core: 2. Of those that a mesh axis runs over, the one named last changes fastest.
Arguments:
- tokens: bfloat16 [65536, 2048], P(('dp', 'expert')), may hold values from -6 to 6
- probe: bfloat16 [65536, 2048], P(('dp', 'expert')), may hold values from -20 to 20
- domain: int32 [65536], P(('dp', 'expert')), may hold values from 0 to 21
- mix: float32 [22], replicated, may hold values from 0.5 to 2
- router: bfloat16 [2048, 32], replicated, may hold values from -0.125 to 0.125
- picks: int32 [128, 32, 40], P(('dp', 'expert')), may hold values from 0 to 511, as said below
- w_gate: bfloat16 [2048, 32, 768], P(None, 'expert'), may hold values from -0.125 to 0.125
- w_up: bfloat16 [2048, 32, 768], P(None, 'expert'), may hold values from -0.125 to 0.125
- w_down: bfloat16 [2048, 32, 768], P(None, 'expert'), may hold values from -0.21875 to 0.21875
Outputs:
- domain_loss: float32 [22], replicated
- router_grad: float32 [2048, 32], replicated
- grad_gate: bfloat16 [2048, 32, 768], P('dp', 'expert')
- grad_up: bfloat16 [2048, 32, 768], P('dp', 'expert')
- grad_down: bfloat16 [2048, 32, 768], P('dp', 'expert')
Inputs may be any that keep to these rules, and one draw needn't show every extreme that they name: The 40 picks of one expert on one device are distinct token positions of that device.
All inputs are finite; a program needn't handle non-finite values.
Results may differ from a plain program's by a relative error of at most 0.018.
Values may be sent and summed in bfloat16 or wider, within the bound.
A program may use at most 192 MiB of HBM per device.

v0:
```python
import math
import jax
import jax.numpy as jnp
from jax import lax
from jax.sharding import PartitionSpec as P


def body(tokens, probe, domain, mix, router, picks, w_gate, w_up, w_down):
    token_count, model_width = tokens.shape
    expert_count = router.shape[1]
    slot_count = picks.shape[2]
    domain_count = mix.shape[0]
    data_devices = lax.axis_size("dp")
    expert_devices = lax.axis_size("expert")
    chosen = picks[0]
    logits = jnp.dot(tokens, router, preferred_element_type=jnp.float32)
    gate_vals = jax.nn.sigmoid(jnp.take_along_axis(logits.T, chosen, axis=1))
    outgoing = tokens[chosen].reshape(expert_count, 1, slot_count, model_width)
    received = lax.all_to_all(outgoing, "expert", split_axis=0, concat_axis=1, tiled=True)
    pre_gate = jnp.einsum("jsrd,djf->jsrf", received, w_gate, preferred_element_type=jnp.float32)
    pre_up = jnp.einsum("jsrd,djf->jsrf", received, w_up, preferred_element_type=jnp.float32)
    expert_hidden = (jax.nn.silu(pre_gate) * pre_up).astype(jnp.bfloat16)
    result = jnp.einsum(
        "jsrf,djf->jsrd", expert_hidden, w_down, preferred_element_type=jnp.float32
    ).astype(jnp.bfloat16)
    returned = lax.all_to_all(result, "expert", split_axis=1, concat_axis=0, tiled=True)
    returned, arrived, pre_gate, pre_up, hidden = (
        returned,
        received,
        pre_gate,
        pre_up,
        expert_hidden,
    )
    outputs = returned.reshape(expert_count, slot_count, model_width).astype(jnp.float32)
    contrib = gate_vals[:, :, None] * outputs
    flat_index = chosen.reshape(-1)
    added = (
        jnp.zeros((token_count, model_width), jnp.float32)
        .at[flat_index]
        .add(contrib.reshape(-1, model_width))
    )
    layer_out = tokens.astype(jnp.float32) + added
    difference = layer_out - probe.astype(jnp.float32)
    per_token = jnp.sum(difference * difference, axis=1)
    member = (domain[:, None] == jnp.arange(domain_count, dtype=jnp.int32)[None, :]).astype(
        jnp.float32
    )
    local_loss = jnp.sum(per_token[:, None] * member, axis=0)
    loss_total = lax.psum(local_loss, ("dp", "expert"))
    total_tokens = token_count * data_devices * expert_devices
    loss_scale = 1.0 / math.sqrt(data_devices * expert_devices * slot_count)
    weight_tok = jnp.sum(member * mix[None, :], axis=1)
    upstream = (loss_scale * weight_tok)[:, None] * difference
    picked_up = upstream[chosen]
    gate_slope = jnp.sum(picked_up * outputs, axis=2)
    logit_grad = gate_slope * gate_vals * (1.0 - gate_vals)
    expert_ids = jnp.broadcast_to(jnp.arange(expert_count, dtype=jnp.int32)[:, None], chosen.shape)
    placed = (
        jnp.zeros((token_count, expert_count), jnp.float32).at[chosen, expert_ids].set(logit_grad)
    )
    router_part = jnp.dot(tokens.astype(jnp.float32).T, placed, precision=lax.Precision.HIGHEST)
    sending = (
        (gate_vals[:, :, None] * picked_up)
        .astype(jnp.bfloat16)
        .reshape(expert_count, 1, slot_count, model_width)
    )
    back_grad = lax.all_to_all(sending, "expert", split_axis=0, concat_axis=1, tiled=True)
    hidden_grad = jnp.einsum(
        "jsrd,djf->jsrf", back_grad, w_down, preferred_element_type=jnp.float32
    )
    sigmoid_gate = jax.nn.sigmoid(pre_gate)
    gate_in = (
        hidden_grad * pre_up * sigmoid_gate * (1.0 + pre_gate * (1.0 - sigmoid_gate))
    ).astype(jnp.bfloat16)
    up_in = (hidden_grad * jax.nn.silu(pre_gate)).astype(jnp.bfloat16)

    def input_term(grads_in):
        return jnp.einsum("jsrd,jsrf->djf", arrived, grads_in, preferred_element_type=jnp.float32)

    grad_gate = lax.psum_scatter(
        input_term(gate_in).astype(jnp.bfloat16), "dp", scatter_dimension=0, tiled=True
    )
    grad_up = lax.psum_scatter(
        input_term(up_in).astype(jnp.bfloat16), "dp", scatter_dimension=0, tiled=True
    )
    grad_down = lax.psum_scatter(
        jnp.einsum("jsrd,jsrf->djf", back_grad, hidden, preferred_element_type=jnp.float32).astype(
            jnp.bfloat16
        ),
        "dp",
        scatter_dimension=0,
        tiled=True,
    )
    router_total = lax.psum(router_part, ("dp", "expert"))
    domain_loss = loss_total * (domain_count / (total_tokens * model_width))
    return (domain_loss, router_total, grad_gate, grad_up, grad_down)


def solution(mesh):
    placed = (
        P(("dp", "expert"), None),
        P(("dp", "expert"), None),
        P(("dp", "expert")),
        P(),
        P(),
        P(("dp", "expert"), None, None),
        P(None, "expert", None),
        P(None, "expert", None),
        P(None, "expert", None),
    )
    return jax.shard_map(
        body,
        mesh=mesh,
        in_specs=placed,
        out_specs=(
            P(),
            P(),
            P("dp", "expert", None),
            P("dp", "expert", None),
            P("dp", "expert", None),
        ),
        check_vma=False,
    )
```

profile of v0, /device:TPU:1, one launch (start us, length us, event | category | flops | bytes accessed | tf_op | source)
XLA Modules:
  0.0 717.0 jit_solution(11860185707785233741)
XLA Ops:
  8.9 12.7 %gather_fusion = bf16[1280,2048]{1,0:T(8,128)(2,1)} fusion(bf16[512,2048]{1,0:T(8,128)(2,1)} %param.9, s32[2048]{0:T(1024)S(1)} %pad_clamp_fusion), kind=kCustom, calls=%fused_computation | custom fusion | bytes 10490880 | tf_op jit(solution)/shard_map/gather | solution.py:18
  21.6 71.7 %all_to_all.45 = bf16[32,1,40,2048]{3,2,1,0:T(8,128)(2,1)S(1)} all-to-all(bf16[32,1,40,2048]{3,2,1,0:T(8,128)(2,1)} %bitcast.90), channel_id=1, replica_groups=mesh['dp'=8,'expert'=16] {'expert'}, dimensions={0} | all-to-all | bytes 10485760 | tf_op jit(solution)/shard_map/all_to_all | solution.py:19
  93.3 4.4 fusion.6
  97.7 6.5 multiply_convert_fusion.3
  104.3 7.7 %fusion.20 = bf16[2,16,40,2048]{3,2,1,0:T(8,128)(2,1)S(1)} fusion(bf16[2,16,40,768]{3,2,1,0:T(8,128)(2,1)} %get-tuple-element.36, bf16[2048,2,768,1]{2,1,0,3:T(2,128)(2,1)} %bitcast.102), kind=kOutput, calls=%fused_computation.34 | convolution fusion | flops 4029153280 | bytes 13500416 | tf_op jit(solution)/shard_map/jsrf,djf->jsrd/dot_general | solution.py:23
  111.9 2.7 copy.64
  114.7 5.6 all-to-all-start.1
  121.0 2.5 convert_element_type.66
  124.4 10.1 %gather_fusion.2 = f32[1280]{0:T(1024)S(1)} fusion(f32[32,512]{1,0:T(8,128)S(1)} %fusion.36, s32[1280]{0:T(1024)S(1)} %reshape.165), kind=kCustom, calls=%fused_computation.2 | custom fusion | bytes 20480 | tf_op jit(solution)/shard_map/jit(take_along_axis)/gather | solution.py:17
  134.7 55.0 %all-to-all-done.1 = bf16[2,16,40,2048]{3,2,0,1:T(8,128)(2,1)} async-done(((bf16[2,16,40,2048]{3,2,0,1:T(8,128)(2,1)}), bf16[2,16,40,2048]{3,2,0,1:T(8,128)(2,1)}, u32[]{:S(2)}, u32[]{:S(2)}) %all-to-all-start.1) | async-done | bytes 5242912 | tf_op jit(solution)/shard_map/all_to_all | solution.py:26
  189.7 3.9 bitcast_convert_fusion.3
  193.5 4.6 bitcast_multiply_fusion
  198.2 25.3 %scatter_fusion = f32[512,2048]{1,0:T(8,128)} fusion(f32[512,2048]{1,0:T(8,128)} %convert_element_type.66, s32[1280]{0:T(1024)S(1)} %fusion.33, f32[1280,2048]{1,0:T(8,128)} %bitcast_multiply_fusion), kind=kCustom, calls=%fused_computation.3 | custom fusion | flops 2621440 | bytes 31462400 | tf_op jit(solution)/shard_map/scatter-add | solution.py:40
  223.6 3.0 multiply_reduce_fusion
  227.0 2.5 fusion.28
  229.5 13.0 %gather_fusion.1 = f32[1280,2048]{1,0:T(8,128)} fusion(f32[512,2048]{1,0:T(8,128)} %fusion.28, s32[2048]{0:T(1024)S(1)} %pad_clamp_fusion), kind=kCustom, calls=%fused_computation.1 | custom fusion | bytes 20976640 | tf_op jit(solution)/shard_map/gather | solution.py:54
  242.5 6.7 fusion
  251.0 2.9 multiply_convert_fusion
  253.9 76.7 %all_to_all.46 = bf16[32,1,40,2048]{3,2,1,0:T(8,128)(2,1)S(1)} all-to-all(bf16[32,1,40,2048]{3,2,1,0:T(8,128)(2,1)} %multiply_convert_fusion), channel_id=1, replica_groups=mesh['dp'=8,'expert'=16] {'expert'}, dimensions={0} | all-to-all | bytes 10485760 | tf_op jit(solution)/shard_map/all_to_all | solution.py:67
  330.5 2.3 copy-done.8
  332.8 7.1 fusion.3
  340.2 8.2 %fusion.8 = f32[2,16,40,768]{3,2,1,0:T(8,128)S(1)} fusion(bf16[2048,2,768,1]{2,1,0,3:T(2,128)(2,1)} %bitcast.103, bf16[16,2,1,40,2048]{4,3,1,0,2:T(8,128)(2,1)} %bitcast.96), kind=kOutput, calls=%fused_computation.19 | convolution fusion | flops 4026531840 | bytes 15466496 | tf_op jit(solution)/shard_map/jsrd,djf->jsrf/dot_general | solution.py:68
  348.4 1.9 copy-done.19
  350.4 9.9 %fusion.2 = bf16[2048,2,768]{0,2,1:T(8,128)(2,1)} fusion(bf16[16,2,1,40,2048]{4,3,1,0,2:T(8,128)(2,1)} %bitcast.93, f32[2,16,40,768]{3,2,1,0:T(8,128)S(1)} %fusion.8, f32[2,16,40,768]{3,2,1,0:T(8,128)S(1)} %copy-done.18), kind=kOutput, calls=%fused_computation.13 | convolution fusion | flops 4035575808 | bytes 19398656 | tf_op jit(solution)/shard_map/jsrd,jsrf->djf/dot_general | solution.py:78
  360.3 12.5 %fusion.1 = bf16[2048,2,768]{0,2,1:T(8,128)(2,1)} fusion(bf16[16,2,1,40,2048]{4,3,1,0,2:T(8,128)(2,1)} %bitcast.94, f32[2,16,40,768]{3,2,1,0:T(8,128)} %copy-done.17, f32[2,16,40,768]{3,2,1,0:T(8,128)} %copy-done.19, f32[2,16,40,768]{3,2,1,0:T(8,128)} %get-tuple-element.37), kind=kOutput, calls=%fused_computation.12 | convolution fusion | flops 4039507968 | bytes 23330816 | tf_op jit(solution)/shard_map/jsrd,jsrf->djf/dot_general | solution.py:78
  373.8 187.1 %psum.14 = f32[22]{0:T(128)S(1)} all-reduce(f32[22]{0:T(128)S(1)} %get-tuple-element.31), channel_id=1, replica_groups=mesh['dp'=8,'expert'=16] {'dp','expert'}, use_global_device_ids=true, to_apply=%region_3.4 | all-reduce | flops 22 | bytes 176 | tf_op jit(solution)/shard_map/psum | solution.py:49
  561.0 5.3 scatter_custom_fusion.1
  566.3 1.8 convolution_bitcast_fusion
  568.7 3.0 copy.72
  571.7 3.0 copy.71
  574.8 3.0 copy.70
  577.8 130.2 %all-reduce.2.cloned.1.call-done = f32[2048,32]{0,1:T(8,128)} async-done(((f32[2048,32]{0,1:T(8,128)}), f32[2048,32]{0,1:T(8,128)}) %all-reduce.2.cloned.1.call-update) | async-done | bytes 262160 | tf_op jit(solution)/shard_map/psum | solution.py:94
  (78 shorter events, 8.3 us)
Async XLA Ops:
  8.0 115.7 %copy-start = (bf16[2048,32]{0,1:T(8,128)(2,1)S(1)}, bf16[2048,32]{0,1:T(8,128)(2,1)}, u32[]{:S(2)}) copy-start(bf16[2048,32]{0,1:T(8,128)(2,1)} %param.13) | copy-start | bytes 393220
  8.8 12.8 %copy-start.10 = (s32[32,40,1]{1,0,2:T(8,128)}, s32[32,40,1]{1,0,2:T(8,128)S(1)}, u32[]{:S(2)}) copy-start(s32[32,40,1]{1,0,2:T(8,128)S(1)} %get-tuple-element.35) | copy-start | bytes 15364
  21.6 71.7 %copy-start.16 = (bf16[2048,2,768]{2,1,0:T(2,128)(2,1)S(1)}, bf16[2048,2,768]{2,1,0:T(2,128)(2,1)}, u32[]{:S(2)}) copy-start(bf16[2048,2,768]{2,1,0:T(2,128)(2,1)} %param.15) | copy-start | bytes 18874372
  21.6 76.1 %slice-start = ((s8[6291456]{0:T(1024)(128)(4,1)}), s8[4194304]{0:T(1024)(128)(4,1)S(1)}, s32[]{:S(2)}) async-start(s8[6291456]{0:T(1024)(128)(4,1)} %bitcast.99), calls=%async_computation.10 | async-start | bytes 8388608
  93.3 4.4 copy-start.7
  93.3 4.4 slice-start.1
  97.7 6.6 copy-start.17
  114.7 6.2 copy-start.9
  114.7 6.3 copy-start.3
  114.7 75.0 %all-to-all-start.1 = ((bf16[2,16,40,2048]{3,2,0,1:T(8,128)(2,1)}), bf16[2,16,40,2048]{3,2,0,1:T(8,128)(2,1)}, u32[]{:S(2)}, u32[]{:S(2)}) async-start(bf16[2,16,40,2048]{3,2,0,1:T(8,128)(2,1)} %copy.64), calls=%async_computation.1 | async-start | bytes 10485760 | tf_op jit(solution)/shard_map/all_to_all | solution.py:26
  120.3 448.4 %reduce-scatter.8.cloned.1.call-start = ((), (), s32[]{:S(2)}) async-start(), calls=%async_computation.9 | async-start | bytes 7077888 | tf_op jit(solution)/shard_map/reduce_scatter | solution.py:86
  198.2 25.3 %copy-start.6 = (bf16[512,2048]{1,0:T(8,128)(2,1)S(1)}, bf16[512,2048]{1,0:T(8,128)(2,1)}, u32[]{:S(2)}) copy-start(bf16[512,2048]{1,0:T(8,128)(2,1)} %param.10) | copy-start | bytes 6291460
  223.5 3.0 copy-start.12
  223.6 3.0 copy-start.15
  223.6 3.5 copy-start.2
  242.5 8.5 %copy-start.5 = (f32[1280,2048]{1,0:T(8,128)S(1)}, f32[1280,2048]{1,0:T(8,128)}, u32[]{:S(2)}) copy-start(f32[1280,2048]{1,0:T(8,128)} %gather_fusion.1) | copy-start | bytes 31457284
  253.9 79.0 %copy-start.20 = (bf16[2,16,40,768]{3,2,1,0:T(8,128)(2,1)S(1)}, bf16[2,16,40,768]{3,2,1,0:T(8,128)(2,1)}, u32[]{:S(2)}) copy-start(bf16[2,16,40,768]{3,2,1,0:T(8,128)(2,1)} %get-tuple-element.36) | copy-start | bytes 5898244
  330.5 2.3 copy-start.8
  340.0 231.8 %reduce-scatter.6.cloned.1.call-start = ((), (), s32[]{:S(2)}) async-start(), calls=%async_computation.8 | async-start | bytes 7077888 | tf_op jit(solution)/shard_map/reduce_scatter | solution.py:83
  340.2 10.1 %copy-start.18 = (f32[2,16,40,768]{3,2,1,0:T(8,128)S(1)}, f32[2,16,40,768]{3,2,1,0:T(8,128)}, u32[]{:S(2)}) copy-start(f32[2,16,40,768]{3,2,1,0:T(8,128)} %copy-done.17) | copy-start | bytes 11796484
  348.4 1.9 copy-start.19
  360.3 214.5 %reduce-scatter.4.cloned.1.call-start = ((), (), s32[]{:S(2)}) async-start(), calls=%async_computation.7 | async-start | bytes 7077888 | tf_op jit(solution)/shard_map/reduce_scatter | solution.py:80
  372.8 0.7 copy-start.11
  372.8 0.7 copy-start.13
  372.8 0.8 copy-start.14
  372.8 193.5 %copy-start.4 = (bf16[512,2048]{1,0:T(8,128)(2,1)S(1)}, bf16[512,2048]{1,0:T(8,128)(2,1)}, u32[]{:S(2)}) copy-start(bf16[512,2048]{1,0:T(8,128)(2,1)} %param.9) | copy-start | bytes 6291460
  372.8 336.8 %copy-start.1 = (bf16[2048,32]{0,1:T(8,128)(2,1)S(1)}, bf16[2048,32]{0,1:T(8,128)(2,1)}, u32[]{:S(2)}) copy-start(bf16[2048,32]{0,1:T(8,128)(2,1)} %param.13) | copy-start | bytes 393220
  372.9 335.1 %all-reduce.2.cloned.1.call-start = ((), (), s32[]{:S(2)}) async-start(), calls=%async_computation.6 | async-start | bytes 524288 | tf_op jit(solution)/shard_map/psum | solution.py:94
Sparse Core Ops, SparseCore 0:
  340.1 71.2 reduce-scatter.7
  413.8 71.8 reduce-scatter.5
  488.1 72.0 reduce-scatter.3
Sparse Core Ops, SparseCore 1:
  568.3 139.7 all-reduce.1
where the time goes:
time: 720 us; the launch traced here: 717 us
  blocking collectives  336 us (47%)
  waiting for transfers between devices  185 us (26%)
  local copies, waits for them, and re-layouts  62.2 us (9%)
  matrix products  58.8 us (8%)
  other arithmetic  53 us (7%)
  between operations  15.7 us (2%)
    psum x1, blocking collectives, body(): loss_total = lax.psum(local_loss, ('dp', 'expert'))  187 us
    psum x1, waiting for transfers between devices, body(): router_total = lax.psum(router_part, ('dp', 'expert'))  130 us
    all_to_all x1, blocking collectives, body(): lax.all_to_all(sending, 'expert', split_axis=0, concat_axis=1, tiled=True)  76.7 us
    all_to_all x1, blocking collectives, body(): lax.all_to_all(outgoing, 'expert', split_axis=0, concat_axis=1, tiled=True)  71.7 us
    all_to_all x1, waiting for transfers between devices, body(): lax.all_to_all(result, 'expert', split_axis=1, concat_axis=0, tiled=True)  55 us
    scatter-add x1, other arithmetic, body(): added = jnp.zeros((token_count, model_width), jnp.float32).at[flat_index]...  25.3 us
    unnamed x53, local copies, waits for them, and re-layouts  23.1 us
    dot_general x2, matrix products, input_term(): jnp.einsum('jsrd,jsrf->djf', arrived, grads_in, preferred_element_type=jn...  22.4 us
  transfers between devices with their start and end apart: 5, of which 2 were waited for; matrix products, arithmetic and copies ran while one was open for 9% of the time, Pallas kernels for 0%

commit v1 on v0

--- a/solution.py
+++ b/solution.py
@@ -91,7 +91,7 @@
         scatter_dimension=0,
         tiled=True,
     )
-    router_total = lax.psum(router_part, ("dp", "expert"))
+    router_total = lax.psum(lax.psum(router_part, "expert"), "dp")
     domain_loss = loss_total * (domain_count / (total_tokens * model_width))
     return (domain_loss, router_total, grad_gate, grad_up, grad_down)
 

time: 720 us -> 669 us (0.929)
  blocking collectives: 336 us -> 223 us
  waiting for transfers between devices: 185 us -> 225 us
  starting transfers between devices: 6.54 us -> 21.6 us
    all_to_all x1 -> x0, blocking collectives: 76.7 us -> none  [body(): lax.all_to_all(sending, 'expert', split_axis=0, concat_axis=1, tiled=True)]
    all_to_all x0 -> x1, waiting for transfers between devices: none -> 64.7 us  [body(): lax.all_to_all(sending, 'expert', split_axis=0, concat_axis=1, tiled=True)]
    psum x1, blocking collectives: 187 us -> 152 us  [body(): loss_total = lax.psum(local_loss, ('dp', 'expert'))]
    psum x1 -> x2, waiting for transfers between devices: 130 us -> 105 us  [body(): router_total = lax.psum(lax.psum(router_part, 'expert'), 'dp')]
    all_to_all x0 -> x1, starting transfers between devices: none -> 14.8 us  [body(): lax.all_to_all(sending, 'expert', split_axis=0, concat_axis=1, tiled=True)]
    unnamed x53 -> x47, local copies, waits for them, and re-layouts: 23.1 us -> 20.9 us
  transfers between devices with their start and end apart: 5 -> 7, of which waited for: 2 -> 4; matrix products, arithmetic and copies ran while one was open for 9% -> 11% of each run, Pallas kernels for 0% -> 0%
where the time goes in v1:
time: 669 us; the launch traced here: 661 us
  waiting for transfers between devices  225 us (34%)
  blocking collectives  223 us (33%)
  matrix products  61.2 us (9%)
  local copies, waits for them, and re-layouts  59.9 us (9%)
  other arithmetic  54 us (8%)
  starting transfers between devices  21.6 us (3%)
  between operations  16.2 us (2%)
    psum x1, blocking collectives, body(): loss_total = lax.psum(local_loss, ('dp', 'expert'))  152 us
    psum x2, waiting for transfers between devices, body(): router_total = lax.psum(lax.psum(router_part, 'expert'), 'dp')  105 us
    all_to_all x1, blocking collectives, body(): lax.all_to_all(outgoing, 'expert', split_axis=0, concat_axis=1, tiled=True)  71.7 us
    all_to_all x1, waiting for transfers between devices, body(): lax.all_to_all(sending, 'expert', split_axis=0, concat_axis=1, tiled=True)  64.7 us
    all_to_all x1, waiting for transfers between devices, body(): lax.all_to_all(result, 'expert', split_axis=1, concat_axis=0, tiled=True)  55.4 us
    scatter-add x1, other arithmetic, body(): added = jnp.zeros((token_count, model_width), jnp.float32).at[flat_index]...  25.3 us
    dot_general x2, matrix products, input_term(): jnp.einsum('jsrd,jsrf->djf', arrived, grads_in, preferred_element_type=jn...  22.1 us
    unnamed x47, local copies, waits for them, and re-layouts  20.9 us
  transfers between devices with their start and end apart: 7, of which 4 were waited for; matrix products, arithmetic and copies ran while one was open for 11% of the time, Pallas kernels for 0%

profile of v1, /device:TPU:1, one launch (start us, length us, event | category | flops | bytes accessed | tf_op | source)
XLA Modules:
  0.0 661.4 jit_solution(14163249834587271281)
XLA Ops:
  8.9 12.7 %gather_fusion = bf16[1280,2048]{1,0:T(8,128)(2,1)} fusion(bf16[512,2048]{1,0:T(8,128)(2,1)} %param.9, s32[2048]{0:T(1024)S(1)} %pad_clamp_fusion), kind=kCustom, calls=%fused_computation | custom fusion | bytes 10490880 | tf_op jit(solution)/shard_map/gather | solution.py:18
  21.6 71.7 %all_to_all.45 = bf16[32,1,40,2048]{3,2,1,0:T(8,128)(2,1)S(1)} all-to-all(bf16[32,1,40,2048]{3,2,1,0:T(8,128)(2,1)} %bitcast.90), channel_id=1, replica_groups=mesh['dp'=8,'expert'=16] {'expert'}, dimensions={0} | all-to-all | bytes 10485760 | tf_op jit(solution)/shard_map/all_to_all | solution.py:19
  93.3 4.4 fusion.6
  97.7 6.5 multiply_convert_fusion.3
  104.2 7.7 %fusion.20 = bf16[2,16,40,2048]{3,2,1,0:T(8,128)(2,1)S(1)} fusion(bf16[2,16,40,768]{3,2,1,0:T(8,128)(2,1)} %get-tuple-element.36, bf16[2048,2,768,1]{2,1,0,3:T(2,128)(2,1)} %bitcast.100), kind=kOutput, calls=%fused_computation.34 | convolution fusion | flops 4029153280 | bytes 13500416 | tf_op jit(solution)/shard_map/jsrf,djf->jsrd/dot_general | solution.py:23
  111.9 2.7 copy.64
  114.6 6.3 all-to-all-start.1
  121.1 2.6 convert_element_type.66
  124.6 10.1 %gather_fusion.2 = f32[1280]{0:T(1024)S(1)} fusion(f32[32,512]{1,0:T(8,128)S(1)} %fusion.36, s32[1280]{0:T(1024)S(1)} %reshape.165), kind=kCustom, calls=%fused_computation.2 | custom fusion | bytes 20480 | tf_op jit(solution)/shard_map/jit(take_along_axis)/gather | solution.py:17
  134.9 55.4 %all-to-all-done.1 = bf16[2,16,40,2048]{3,2,0,1:T(8,128)(2,1)} async-done(((bf16[2,16,40,2048]{3,2,0,1:T(8,128)(2,1)}), bf16[2,16,40,2048]{3,2,0,1:T(8,128)(2,1)}, u32[]{:S(2)}, u32[]{:S(2)}) %all-to-all-start.1) | async-done | bytes 5242912 | tf_op jit(solution)/shard_map/all_to_all | solution.py:26
  190.2 3.9 bitcast_convert_fusion.3
  194.1 4.7 bitcast_multiply_fusion
  198.9 25.3 %scatter_fusion = f32[512,2048]{1,0:T(8,128)} fusion(f32[512,2048]{1,0:T(8,128)} %convert_element_type.66, s32[1280]{0:T(1024)S(1)} %fusion.33, f32[1280,2048]{1,0:T(8,128)} %bitcast_multiply_fusion), kind=kCustom, calls=%fused_computation.3 | custom fusion | flops 2621440 | bytes 31462400 | tf_op jit(solution)/shard_map/scatter-add | solution.py:40
  224.2 3.6 multiply_reduce_fusion
  228.9 2.6 fusion.28
  231.5 13.0 %gather_fusion.1 = f32[1280,2048]{1,0:T(8,128)} fusion(f32[512,2048]{1,0:T(8,128)} %fusion.28, s32[2048]{0:T(1024)S(1)} %pad_clamp_fusion), kind=kCustom, calls=%fused_computation.1 | custom fusion | bytes 20976640 | tf_op jit(solution)/shard_map/gather | solution.py:54
  244.5 6.7 %fusion = f32[16,2,40]{2,1,0:T(2,128)S(1)} fusion(f32[16,2,1,40,2048]{4,3,1,0,2:T(8,128)} %bitcast.88, bf16[2,16,40,2048]{3,2,0,1:T(8,128)(2,1)} %all-to-all-done.1), kind=kLoop, calls=%fused_computation.10 | loop fusion | flops 7863040 | bytes 15733760 | tf_op jit(solution)/shard_map/reduce_sum | solution.py:55
  253.0 2.9 multiply_convert_fusion
  255.9 14.8 %all-to-all-start.2 = ((bf16[32,1,40,2048]{3,2,1,0:T(8,128)(2,1)}), bf16[32,1,40,2048]{3,2,1,0:T(8,128)(2,1)}, u32[]{:S(2)}, u32[]{:S(2)}) async-start(bf16[32,1,40,2048]{3,2,1,0:T(8,128)(2,1)} %multiply_convert_fusion), calls=%async_computation.2 | async-start | bytes 10485760 | tf_op jit(solution)/shard_map/all_to_all | solution.py:67
  271.1 5.3 scatter_custom_fusion.1
  278.3 64.7 %all-to-all-done.2 = bf16[32,1,40,2048]{3,2,1,0:T(8,128)(2,1)} async-done(((bf16[32,1,40,2048]{3,2,1,0:T(8,128)(2,1)}), bf16[32,1,40,2048]{3,2,1,0:T(8,128)(2,1)}, u32[]{:S(2)}, u32[]{:S(2)}) %all-to-all-start.2) | async-done | bytes 5242912 | tf_op jit(solution)/shard_map/all_to_all | solution.py:67
  343.0 9.8 %fusion.3 = bf16[2048,2,768]{0,2,1:T(8,128)(2,1)} fusion(bf16[2,16,40,768]{3,2,1,0:T(8,128)(2,1)} %get-tuple-element.36, bf16[16,2,1,40,2048]{4,3,1,0,2:T(8,128)(2,1)} %bitcast.20), kind=kOutput, calls=%fused_computation.14 | convolution fusion | flops 4029677568 | bytes 13500416 | tf_op jit(solution)/shard_map/jsrd,jsrf->djf/dot_general | solution.py:87
  353.1 8.2 %fusion.8 = f32[2,16,40,768]{3,2,1,0:T(8,128)S(1)} fusion(bf16[2048,2,768,1]{2,1,0,3:T(2,128)(2,1)} %bitcast.101, bf16[16,2,1,40,2048]{4,3,1,0,2:T(8,128)(2,1)} %bitcast.20), kind=kOutput, calls=%fused_computation.19 | convolution fusion | flops 4026531840 | bytes 15466496 | tf_op jit(solution)/shard_map/jsrd,djf->jsrf/dot_general | solution.py:68
  361.3 2.0 copy-done.17
  363.3 9.9 %fusion.2 = bf16[2048,2,768]{0,2,1:T(8,128)(2,1)} fusion(bf16[16,2,1,40,2048]{4,3,1,0,2:T(8,128)(2,1)} %bitcast.93, f32[2,16,40,768]{3,2,1,0:T(8,128)S(1)} %fusion.8, f32[2,16,40,768]{3,2,1,0:T(8,128)S(1)} %copy-done.16), kind=kOutput, calls=%fused_computation.13 | convolution fusion | flops 4035575808 | bytes 19398656 | tf_op jit(solution)/shard_map/jsrd,jsrf->djf/dot_general | solution.py:78
  373.3 12.3 %fusion.1 = bf16[2048,2,768]{0,2,1:T(8,128)(2,1)} fusion(bf16[16,2,1,40,2048]{4,3,1,0,2:T(8,128)(2,1)} %bitcast.94, f32[2,16,40,768]{3,2,1,0:T(8,128)} %copy-done.15, f32[2,16,40,768]{3,2,1,0:T(8,128)} %copy-done.17, f32[2,16,40,768]{3,2,1,0:T(8,128)} %get-tuple-element.37), kind=kOutput, calls=%fused_computation.12 | convolution fusion | flops 4039507968 | bytes 23330816 | tf_op jit(solution)/shard_map/jsrd,jsrf->djf/dot_general | solution.py:78
  385.6 91.3 %all-reduce.3.cloned.1.call-done = f32[2048,32]{0,1:T(8,128)} async-done(((f32[2048,32]{0,1:T(8,128)}), f32[2048,32]{0,1:T(8,128)}) %all-reduce.3.cloned.1.call-update) | async-done | bytes 262160 | tf_op jit(solution)/shard_map/psum | solution.py:94
  476.9 151.6 %psum.21 = f32[22]{0:T(128)S(1)} all-reduce(f32[22]{0:T(128)S(1)} %get-tuple-element.31), channel_id=1, replica_groups=mesh['dp'=8,'expert'=16] {'dp','expert'}, use_global_device_ids=true, to_apply=%region_3.4 | all-reduce | flops 22 | bytes 176 | tf_op jit(solution)/shard_map/psum | solution.py:49
  629.0 3.0 copy.72
  632.1 3.0 copy.71
  635.1 3.0 copy.70
  638.1 13.8 %all-reduce.5.cloned.1.call-done = f32[2048,32]{0,1:T(8,128)} async-done(((f32[2048,32]{0,1:T(8,128)}), f32[2048,32]{0,1:T(8,128)}) %all-reduce.5.cloned.1.call-update) | async-done | bytes 262160 | tf_op jit(solution)/shard_map/psum | solution.py:94
  (76 shorter events, 9.7 us)
Async XLA Ops:
  8.0 115.9 %copy-start = (bf16[2048,32]{0,1:T(8,128)(2,1)S(1)}, bf16[2048,32]{0,1:T(8,128)(2,1)}, u32[]{:S(2)}) copy-start(bf16[2048,32]{0,1:T(8,128)(2,1)} %param.13) | copy-start | bytes 393220
  8.8 12.8 %copy-start.8 = (s32[32,40,1]{1,0,2:T(8,128)}, s32[32,40,1]{1,0,2:T(8,128)S(1)}, u32[]{:S(2)}) copy-start(s32[32,40,1]{1,0,2:T(8,128)S(1)} %get-tuple-element.35) | copy-start | bytes 15364
  21.6 71.7 %copy-start.14 = (bf16[2048,2,768]{2,1,0:T(2,128)(2,1)S(1)}, bf16[2048,2,768]{2,1,0:T(2,128)(2,1)}, u32[]{:S(2)}) copy-start(bf16[2048,2,768]{2,1,0:T(2,128)(2,1)} %param.15) | copy-start | bytes 18874372
  21.6 76.1 %slice-start = ((s8[6291456]{0:T(1024)(128)(4,1)}), s8[4194304]{0:T(1024)(128)(4,1)S(1)}, s32[]{:S(2)}) async-start(s8[6291456]{0:T(1024)(128)(4,1)} %bitcast.97), calls=%async_computation.11 | async-start | bytes 8388608
  93.3 4.4 copy-start.6
  93.3 4.4 slice-start.1
  97.6 6.6 copy-start.15
  114.6 6.3 copy-start.7
  114.6 6.4 copy-start.3
  114.6 75.6 %all-to-all-start.1 = ((bf16[2,16,40,2048]{3,2,0,1:T(8,128)(2,1)}), bf16[2,16,40,2048]{3,2,0,1:T(8,128)(2,1)}, u32[]{:S(2)}, u32[]{:S(2)}) async-start(bf16[2,16,40,2048]{3,2,0,1:T(8,128)(2,1)} %copy.64), calls=%async_computation.1 | async-start | bytes 10485760 | tf_op jit(solution)/shard_map/all_to_all | solution.py:26
  198.9 29.0 %copy-start.13 = (f32[22]{0:T(128)S(1)}, f32[22]{0:T(128)}, u32[]{:S(2)}) copy-start(f32[22]{0:T(128)} %param.12) | copy-start | bytes 268
  224.2 3.7 copy-start.10
  224.2 4.1 copy-start.2
  224.2 4.7 copy-start.5
  244.5 8.5 %copy-start.4 = (f32[1280,2048]{1,0:T(8,128)S(1)}, f32[1280,2048]{1,0:T(8,128)}, u32[]{:S(2)}) copy-start(f32[1280,2048]{1,0:T(8,128)} %gather_fusion.1) | copy-start | bytes 31457284
  255.9 14.9 %copy-start.9 = (s32[32,40,1]{1,0,2:T(8,128)S(1)}, s32[32,40,1]{1,0,2:T(8,128)}, u32[]{:S(2)}) copy-start(s32[32,40,1]{1,0,2:T(8,128)} %copy-done.8) | copy-start | bytes 15364
  255.9 14.9 %copy-start.11 = (s32[2]{0:T(128)S(1)}, s32[2]{0:T(128)}, u32[]{:S(2)}) copy-start(s32[2]{0:T(128)} %constant.42) | copy-start | bytes 28
  255.9 15.0 %copy-start.12 = (s32[2]{0:T(128)S(1)}, s32[2]{0:T(128)}, u32[]{:S(2)}) copy-start(s32[2]{0:T(128)} %constant.45) | copy-start | bytes 28
  255.9 87.1 %all-to-all-start.2 = ((bf16[32,1,40,2048]{3,2,1,0:T(8,128)(2,1)}), bf16[32,1,40,2048]{3,2,1,0:T(8,128)(2,1)}, u32[]{:S(2)}, u32[]{:S(2)}) async-start(bf16[32,1,40,2048]{3,2,1,0:T(8,128)(2,1)} %multiply_convert_fusion), calls=%async_computation.2 | async-start | bytes 10485760 | tf_op jit(solution)/shard_map/all_to_all | solution.py:67
  270.7 206.2 %all-reduce.3.cloned.1.call-start = ((), (), s32[]{:S(2)}) async-start(), calls=%async_computation.6 | async-start | bytes 524288 | tf_op jit(solution)/shard_map/psum | solution.py:94
  278.3 350.8 %reduce-scatter.8.cloned.1.call-start = ((), (), s32[]{:S(2)}) async-start(), calls=%async_computation.10 | async-start | bytes 7077888 | tf_op jit(solution)/shard_map/reduce_scatter | solution.py:86
  352.9 279.2 %reduce-scatter.6.cloned.1.call-start = ((), (), s32[]{:S(2)}) async-start(), calls=%async_computation.9 | async-start | bytes 7077888 | tf_op jit(solution)/shard_map/reduce_scatter | solution.py:83
  353.1 10.2 %copy-start.16 = (f32[2,16,40,768]{3,2,1,0:T(8,128)S(1)}, f32[2,16,40,768]{3,2,1,0:T(8,128)}, u32[]{:S(2)}) copy-start(f32[2,16,40,768]{3,2,1,0:T(8,128)} %copy-done.15) | copy-start | bytes 11796484
  361.3 2.0 copy-start.17
  373.2 261.9 %reduce-scatter.4.cloned.1.call-start = ((), (), s32[]{:S(2)}) async-start(), calls=%async_computation.8 | async-start | bytes 7077888 | tf_op jit(solution)/shard_map/reduce_scatter | solution.py:80
  385.5 268.0 %copy-start.1 = (bf16[2048,32]{0,1:T(8,128)(2,1)S(1)}, bf16[2048,32]{0,1:T(8,128)(2,1)}, u32[]{:S(2)}) copy-start(bf16[2048,32]{0,1:T(8,128)(2,1)} %param.13) | copy-start | bytes 393220
  385.6 266.3 %all-reduce.5.cloned.1.call-start = ((), (), s32[]{:S(2)}) async-start(), calls=%async_computation.7 | async-start | bytes 524288 | tf_op jit(solution)/shard_map/psum | solution.py:94
Sparse Core Ops, SparseCore 0:
  278.4 198.4 all-reduce.2
Sparse Core Ops, SparseCore 1:
  352.9 80.5 reduce-scatter.7
  435.8 71.5 reduce-scatter.5
  509.7 71.8 reduce-scatter.3
  584.1 67.7 all-reduce.4
